TPU v7x, 256 devices: a whole 4x4x8 slice. The times are simulated.
256 devices in a mesh: pair: 2 (over y_hi), tm: 128 (over y_lo, x, z, core).
Axes of the slice: x: 4, y: 4 (y_hi: 2, y_lo: 2; y = y_hi * 2 + y_lo), z: 8, core: 2. Of those that a mesh axis runs over, the one named last changes fastest.
Arguments:
- fields: float32 [2, 128, 256, 256], P('pair', 'tm'), may hold values from -4 to 4
- forcing: float32 [2, 128, 256, 256], P('pair', 'tm'), may hold values from -4 to 4.3
- diffusion: float32 [256, 256], replicated, may hold values from 0.5 to 2
- reaction: float32 [256, 256], replicated, may hold values from 0.02 to 0.2
- wrap_factor: float32 [1], replicated, may hold values from 0.05 to 0.4
- mean_diffusion: float32 [1], replicated, may hold values from 0.8 to 1.25
- spectral_shift: float32 [1], replicated, may hold values from 0.05 to 1
Outputs:
- updated: float32 [2, 128, 256, 256], P('pair', 'tm')
All inputs are finite; a program needn't handle non-finite values.
Results may differ from a plain program's by a relative error of at most 0.0003.
Values sent between devices are 32-bit elements; how exact they have to be, the bound alone decides.
A program may use at most 64 MiB of HBM per device.

v0:
```python
import math

import jax
import jax.numpy as jnp
import numpy as np
from jax import lax
from jax.sharding import PartitionSpec as P

ITERS = 2
GAMMA_INV = 0.5


def cas_matrix(length):
    wrapped = np.outer(np.arange(length), np.arange(length)) % length
    angles = wrapped * (2.0 * math.pi / length)
    return ((np.cos(angles) + np.sin(angles)) / math.sqrt(length)).astype(np.float32)


def both_sides(matrix, values):
    left = jnp.dot(values, matrix, precision=lax.Precision.HIGH)
    return jnp.dot(matrix, left, precision=lax.Precision.HIGH)


def spread_of(values, face_x, face_y):
    flux_x = face_x * (jnp.roll(values, -1, 0) - values)
    flux_y = face_y * (jnp.roll(values, -1, 1) - values)
    return flux_x - jnp.roll(flux_x, 1, 0) + flux_y - jnp.roll(flux_y, 1, 1)


def time_sweep(rhs, ratio, alpha, last):
    steps = rhs.shape[0]
    part = ratio * rhs
    power = ratio
    width = 1
    while width < steps:
        moved = jnp.concatenate([jnp.zeros_like(part[:width]), part[:-width]], 0)
        part = part + power * moved
        power = power * power
        width *= 2
    carry = alpha * (part[-1:] - last) / (1.0 - alpha * power)
    ages = jnp.arange(1, steps + 1, dtype=jnp.float32)[:, None]
    decay = jnp.exp(ages * jnp.log(ratio))
    return part + decay * carry


def on_device(fields, forcing, diffusion, reaction, wrap_factor, mean_diffusion, spectral_shift):
    place = lax.axis_index("tm")
    count = lax.axis_size("tm")
    adjoint = lax.axis_index("pair") == 1
    values = fields[0, 0]
    source = forcing[0, 0]
    size = values.shape[0]
    alpha = wrap_factor[0]
    mean = mean_diffusion[0]
    shift = spectral_shift[0]
    face_x = 0.5 * (diffusion + jnp.roll(diffusion, -1, 0)) - mean
    face_y = 0.5 * (diffusion + jnp.roll(diffusion, -1, 1)) - mean
    matrix = jnp.asarray(cas_matrix(size))
    sines = jnp.sin(jnp.arange(size, dtype=jnp.float32) * (math.pi / size)) ** 2
    rows = size // count
    own = lax.dynamic_slice_in_dim(sines, place * rows, rows)
    eigen = 4.0 * own[:, None] + 4.0 * sines[None, :]
    ratio = (1.0 / (1.0 + mean * eigen + shift)).reshape(1, rows * size)
    ends = [(count - 1, 0), (count, 2 * count - 1)]
    wrapped = lax.ppermute(values, ("pair", "tm"), ends)
    last = jnp.zeros_like(ratio)

    for _ in range(ITERS):
        partner = lax.ppermute(values, "pair", [(0, 1), (1, 0)])
        state = reaction * values * values * values + GAMMA_INV * partner
        dual = 3.0 * reaction * partner * partner * values - partner
        coupling = jnp.where(adjoint, dual, state)
        rhs = source + shift * values + spread_of(values, face_x, face_y) - coupling
        rhs = rhs - alpha * wrapped
        modes = both_sides(matrix, rhs).reshape(count, rows * size)
        times = lax.all_to_all(modes, "tm", split_axis=0, concat_axis=0, tiled=True)
        times = jnp.where(adjoint, jnp.flip(times, 0), times)
        times = time_sweep(times, ratio, alpha, last)
        last = times[-1:]
        wrapped = jnp.zeros_like(values)
        times = jnp.where(adjoint, jnp.flip(times, 0), times)
        modes = lax.all_to_all(times, "tm", split_axis=0, concat_axis=0, tiled=True)
        values = both_sides(matrix, modes.reshape(size, size))
    return values[None, None]


def solution(mesh):
    split = P("pair", "tm", None, None)
    return jax.shard_map(
        on_device,
        mesh=mesh,
        in_specs=(split, split, P(), P(), P(), P(), P()),
        out_specs=split,
        check_vma=False,
    )
```

profile of v0, /device:TPU:1, one launch (start us, length us, event | category | flops | bytes accessed | tf_op | source)
XLA Modules:
  0.0 115.4 jit_solution(10037513194033987692)
XLA Ops:
  0.0 3.7 %collective-permute-start = (f32[256,256]{1,0:T(8,128)}, f32[256,256]{1,0:T(8,128)S(1)}, u32[]{:S(2)}, u32[]{:S(2)}) collective-permute-start(f32[256,256]{1,0:T(8,128)} %bitcast.83), channel_id=1, source_target_pairs={{0,128},{128,0},{1,129},{129,1},{2,130},{130,2},{3,131},{131,3},{4... | collective-permute-start | bytes 786440 | tf_op jit(solution)/shard_map/ppermute | solution.py:69
  3.7 0.7 collective-permute-start.1
  4.4 1.1 slice.166
  5.5 0.0 copy-done.1
  5.5 0.0 copy-start.2
  5.5 0.9 copy-done.2
  6.5 0.1 slice.133
  7.3 0.0 copy-start.3
  7.3 0.0 copy-start.4
  7.4 0.2 fusion.20
  7.5 0.0 copy-start
  7.6 0.1 slice.168
  9.0 0.1 dynamic-slice_multiply_fusion
  9.1 0.0 collective-permute-done
  9.1 0.0 collective-permute-done.1
  9.2 0.5 fusion.5
  9.6 0.3 fusion.75
  9.9 1.0 all_to_all.38
  10.9 15.4 %all-to-all-start = ((f32[128,1,512]{2,1,0:T(1,128)}), f32[128,1,512]{2,1,0:T(1,128)S(1)}, u32[]{:S(2)}, u32[]{:S(2)}) async-start(f32[128,1,512]{2,1,0:T(1,128)} %all_to_all.38), calls=%async_computation | async-start | bytes 524288 | tf_op jit(solution)/shard_map/all_to_all | solution.py:76
  26.3 0.1 subtract_bitcast_fusion
  26.4 13.4 %all-to-all-done = f32[128,1,512]{2,1,0:T(1,128)S(1)} async-done(((f32[128,1,512]{2,1,0:T(1,128)}), f32[128,1,512]{2,1,0:T(1,128)S(1)}, u32[]{:S(2)}, u32[]{:S(2)}) %all-to-all-start) | async-done | bytes 262176 | tf_op jit(solution)/shard_map/all_to_all | solution.py:76
  39.8 0.1 rev.13
  40.4 0.1 multiply_add_fusion.8
  40.6 0.1 rev.14
  40.7 0.1 select_bitcast_fusion.1
  40.8 0.3 copy.10
  41.1 19.5 %all_to_all.44 = f32[128,1,512]{2,1,0:T(1,128)S(1)} all-to-all(f32[128,1,512]{2,1,0:T(1,128)S(1)} %copy.10), channel_id=1, replica_groups=mesh['pair'=2,'tm'=128] {'tm'}, dimensions={0} | all-to-all | bytes 524288 | tf_op jit(solution)/shard_map/all_to_all | solution.py:82
  60.6 0.6 reduce
  61.3 0.3 fusion.76
  61.5 0.3 fusion.77
  61.8 3.8 %collective-permute-start.2 = (f32[256,256]{1,0:T(8,128)S(1)}, f32[256,256]{1,0:T(8,128)S(1)}, u32[]{:S(2)}, u32[]{:S(2)}) collective-permute-start(f32[256,256]{1,0:T(8,128)S(1)} %fusion.77), channel_id=1, source_target_pairs={{0,128},{128,0},{1,129},{129,1},{2,130},{130,2},{3,131},{131,3},{4... | collective-permute-start | bytes 786440 | tf_op jit(solution)/shard_map/ppermute | solution.py:69
  65.7 0.1 slice.182
  65.8 0.2 fusion.33
  66.0 0.1 slice.184
  66.1 5.9 %collective-permute-done.2 = f32[256,256]{1,0:T(8,128)S(1)} collective-permute-done((f32[256,256]{1,0:T(8,128)S(1)}, f32[256,256]{1,0:T(8,128)S(1)}, u32[]{:S(2)}, u32[]{:S(2)}) %collective-permute-start.2) | collective-permute-done | bytes 262176 | tf_op jit(solution)/shard_map/ppermute | solution.py:69
  72.0 0.5 fusion.14
  72.5 0.3 fusion.78
  72.7 0.3 all_to_all.39
  73.0 19.6 %all_to_all.45 = f32[128,1,512]{2,1,0:T(1,128)S(1)} all-to-all(f32[128,1,512]{2,1,0:T(1,128)S(1)} %all_to_all.39), channel_id=1, replica_groups=mesh['pair'=2,'tm'=128] {'tm'}, dimensions={0} | all-to-all | bytes 524288 | tf_op jit(solution)/shard_map/all_to_all | solution.py:76
  92.7 0.1 rev.15
  93.3 0.1 multiply_add_fusion
  93.4 0.1 rev.16
  93.6 0.1 select_bitcast_fusion
  93.7 0.3 copy.12
  94.0 19.5 %all_to_all.46 = f32[128,1,512]{2,1,0:T(1,128)S(1)} all-to-all(f32[128,1,512]{2,1,0:T(1,128)S(1)} %copy.12), channel_id=1, replica_groups=mesh['pair'=2,'tm'=128] {'tm'}, dimensions={0} | all-to-all | bytes 524288 | tf_op jit(solution)/shard_map/all_to_all | solution.py:82
  113.5 0.6 reduce.1
  114.1 0.3 fusion.79
  114.4 1.0 convolution_bitcast_fusion
  (51 shorter events, 1.2 us)
Async XLA Ops:
  0.0 5.5 %copy-start.1 = (f32[1,1,256,256]{3,2,1,0:T(8,128)S(1)}, f32[1,1,256,256]{3,2,1,0:T(8,128)}, u32[]{:S(2)}) copy-start(f32[1,1,256,256]{3,2,1,0:T(8,128)} %param.8) | copy-start | bytes 786436
  0.0 9.1 %collective-permute-start = (f32[256,256]{1,0:T(8,128)}, f32[256,256]{1,0:T(8,128)S(1)}, u32[]{:S(2)}, u32[]{:S(2)}) collective-permute-start(f32[256,256]{1,0:T(8,128)} %bitcast.83), channel_id=1, source_target_pairs={{0,128},{128,0},{1,129},{129,1},{2,130},{130,2},{3,131},{131,3},{4... | collective-permute-start | bytes 786440 | tf_op jit(solution)/shard_map/ppermute | solution.py:69
  3.7 5.4 %collective-permute-start.1 = (f32[256,256]{1,0:T(8,128)}, f32[256,256]{1,0:T(8,128)S(1)}, u32[]{:S(2)}, u32[]{:S(2)}) collective-permute-start(f32[256,256]{1,0:T(8,128)} %bitcast.84), channel_id=1, source_target_pairs={{127,0},{128,255}} | collective-permute-start | bytes 786440 | tf_op jit(solution)/shard_map/ppermute | solution.py:65
  5.5 1.0 copy-start.2
  7.3 1.8 %copy-start.3 = (f32[256,256]{1,0:T(8,128)S(1)}, f32[256,256]{1,0:T(8,128)}, u32[]{:S(2)}) copy-start(f32[256,256]{1,0:T(8,128)} %param.11) | copy-start | bytes 786436
  7.3 1.8 %copy-start.4 = (f32[1,1,256,256]{3,2,1,0:T(8,128)S(1)}, f32[1,1,256,256]{3,2,1,0:T(8,128)}, u32[]{:S(2)}) copy-start(f32[1,1,256,256]{3,2,1,0:T(8,128)} %param.9) | copy-start | bytes 786436
  7.5 1.6 %copy-start = (f32[256,256]{1,0:T(8,128)S(1)}, f32[256,256]{1,0:T(8,128)}, u32[]{:S(2)}) copy-start(f32[256,256]{1,0:T(8,128)} %constant.7.clone) | copy-start | bytes 786436
  10.9 28.9 %all-to-all-start = ((f32[128,1,512]{2,1,0:T(1,128)}), f32[128,1,512]{2,1,0:T(1,128)S(1)}, u32[]{:S(2)}, u32[]{:S(2)}) async-start(f32[128,1,512]{2,1,0:T(1,128)} %all_to_all.38), calls=%async_computation | async-start | bytes 524288 | tf_op jit(solution)/shard_map/all_to_all | solution.py:76
  61.8 10.2 %collective-permute-start.2 = (f32[256,256]{1,0:T(8,128)S(1)}, f32[256,256]{1,0:T(8,128)S(1)}, u32[]{:S(2)}, u32[]{:S(2)}) collective-permute-start(f32[256,256]{1,0:T(8,128)S(1)} %fusion.77), channel_id=1, source_target_pairs={{0,128},{128,0},{1,129},{129,1},{2,130},{130,2},{3,131},{131,3},{4... | collective-permute-start | bytes 786440 | tf_op jit(solution)/shard_map/ppermute | solution.py:69
where the time goes:
time: 116 us; the launch traced here: 115 us
  blocking collectives  58.6 us (51%)
  starting transfers between devices  23.6 us (20%)
  waiting for transfers between devices  19.3 us (17%)
  local copies, waits for them, and re-layouts  5.14 us (4%)
  matrix products  3.25 us (3%)
  other arithmetic  2.98 us (3%)
  between operations  2.57 us (2%)
    all_to_all x2, blocking collectives, on_device(): modes = lax.all_to_all(times, 'tm', split_axis=0, concat_axis=0, tiled=True)  38.9 us
    all_to_all x1, blocking collectives, on_device(): times = lax.all_to_all(modes, 'tm', split_axis=0, concat_axis=0, tiled=True)  19.6 us
    all_to_all x1, starting transfers between devices, on_device(): times = lax.all_to_all(modes, 'tm', split_axis=0, concat_axis=0, tiled=True)  15.4 us
    all_to_all x1, waiting for transfers between devices, on_device(): times = lax.all_to_all(modes, 'tm', split_axis=0, concat_axis=0, tiled=True)  13.4 us
    ppermute x2, starting transfers between devices, on_device(): partner = lax.ppermute(values, 'pair', [(0, 1), (1, 0)])  7.57 us
    ppermute x2, waiting for transfers between devices, on_device(): partner = lax.ppermute(values, 'pair', [(0, 1), (1, 0)])  5.9 us
  transfers between devices with their start and end apart: 4, of which 2 were waited for; matrix products, arithmetic and copies ran while one was open for 2% of the time, Pallas kernels for 0%

commit v1 on v0

v1 whole, which is shorter than its diff:
```python
import math

import jax
import jax.numpy as jnp
import numpy as np
from jax import lax
from jax.experimental import pallas as pl
from jax.experimental.pallas import tpu as pltpu
from jax.sharding import PartitionSpec as P

ITERS = 2
GAMMA_INV = 0.5
SIZE = 256
STEPS = 128
SUB = 4
LANES = 128
RUN = 16
MESH = pl.DeviceIdType.MESH


def cas_matrix(length):
    wrapped = np.outer(np.arange(length), np.arange(length)) % length
    angles = wrapped * (2.0 * math.pi / length)
    return (np.cos(angles) + np.sin(angles)) / math.sqrt(length)


def constants():
    matrix = jnp.asarray(cas_matrix(SIZE), jnp.float32)
    high = matrix.astype(jnp.bfloat16)
    low = (matrix - high.astype(jnp.float32)).astype(jnp.bfloat16)
    sines = 4.0 * np.sin(np.arange(SIZE) * (math.pi / SIZE)) ** 2
    eigen = (sines[:, None] + sines[None, :]).astype(np.float32)
    eigen = eigen.reshape(SIZE // SUB, SUB, SIZE // LANES, LANES).transpose(0, 2, 1, 3)
    return high, low, jnp.asarray(eigen.reshape(STEPS, SUB, LANES))


def halves(values):
    high = values.astype(jnp.bfloat16)
    return high, (values - high.astype(jnp.float32)).astype(jnp.bfloat16)


def dot(a, b):
    return jnp.dot(a, b, preferred_element_type=jnp.float32)


def dot_right(values, high, low):
    vh, vl = halves(values)
    return dot(vh, high) + (dot(vl, high) + dot(vh, low))


def dot_left(high, low, values):
    vh, vl = halves(values)
    return dot(high, vh) + (dot(high, vl) + dot(low, vh))


def kernel(
    fields, forcing, diffusion, reaction, alpha_ref, mean_ref, shift_ref, high_in, low_in, eigen,
    out, value, source, diff, react, high, low, eig, partner, wrapped, rhs,
    coef, grid, send, recv, in_sems, pair_send, pair_recv, wrap_sems, all_send, all_recv,
):
    group = lax.axis_index("pair")
    place = lax.axis_index("tm")
    loads = [
        pltpu.make_async_copy(src, dst, in_sems.at[i])
        for i, (src, dst) in enumerate(
            (
                (fields, value), (diffusion, diff), (forcing, source), (reaction, react),
                (high_in, high), (low_in, low), (eigen.at[place], eig),
            )
        )
    ]
    for load in loads:
        load.start()

    barrier = pltpu.get_barrier_semaphore()

    def greet(d, c):
        pl.semaphore_signal(
            barrier, inc=1, device_id={"pair": group, "tm": place ^ (STEPS - d)},
            device_id_type=MESH,
        )
        return c

    pl.semaphore_signal(
        barrier, inc=1, device_id={"pair": 1 - group, "tm": place}, device_id_type=MESH
    )
    lax.fori_loop(1, STEPS, greet, 0)

    alpha = alpha_ref[0]
    mean = mean_ref[0]
    shift = shift_ref[0]
    for load in loads:
        load.wait()

    d = diff[...]
    east = 0.5 * (d + pltpu.roll(d, SIZE - 1, 0)) - mean
    north = 0.5 * (d + pltpu.roll(d, SIZE - 1, 1)) - mean
    west = pltpu.roll(east, 1, 0)
    south = pltpu.roll(north, 1, 1)
    coef[0] = east
    coef[1] = west
    coef[2] = north
    coef[3] = south
    coef[4] = shift - ((east + west) + (north + south))

    def linear_part():
        v = value[...]
        total = source[...] + coef[4] * v
        total += coef[0] * pltpu.roll(v, SIZE - 1, 0) + coef[1] * pltpu.roll(v, 1, 0)
        total += coef[2] * pltpu.roll(v, SIZE - 1, 1) + coef[3] * pltpu.roll(v, 1, 1)
        rhs[...] = total

    lam = 1.0 + mean * eig[...] + shift
    ratio = 1.0 / lam
    run_power = ratio
    for _ in range(4):
        run_power = run_power * run_power
    full_power = run_power
    for _ in range(3):
        full_power = full_power * full_power
    wrap_gain = alpha / (1.0 - alpha * full_power)
    last = jnp.zeros_like(ratio)

    linear_part()
    pl.semaphore_wait(barrier, STEPS)

    is_first = place == (STEPS - 1) * group
    is_last = place == (STEPS - 1) * (1 - group)
    wrap_copy = pltpu.make_async_remote_copy(
        src_ref=value, dst_ref=wrapped, send_sem=wrap_sems.at[0], recv_sem=wrap_sems.at[1],
        device_id={"pair": group, "tm": STEPS - 1 - place}, device_id_type=MESH,
    )

    def exchange(phase):
        def one(d, c):
            peer = place ^ (STEPS - d)
            pltpu.make_async_remote_copy(
                src_ref=send.at[phase % 2, peer], dst_ref=recv.at[phase, place],
                send_sem=all_send.at[phase], recv_sem=all_recv.at[phase],
                device_id={"pair": group, "tm": peer}, device_id_type=MESH,
            ).start()
            return c

        lax.fori_loop(1, STEPS, one, 0)
        recv[phase, place] = send[phase % 2, place]

    def exchange_wait(phase):
        span = pl.ds(0, STEPS - 1)
        wait = pltpu.make_async_remote_copy(
            src_ref=send.at[phase % 2, span], dst_ref=recv.at[phase, span],
            send_sem=all_send.at[phase], recv_sem=all_recv.at[phase],
            device_id={"pair": group, "tm": place}, device_id_type=MESH,
        )
        wait.wait_send()
        wait.wait_recv()

    for it in range(ITERS):
        pair_copy = pltpu.make_async_remote_copy(
            src_ref=value, dst_ref=partner.at[it], send_sem=pair_send.at[it],
            recv_sem=pair_recv.at[it], device_id={"pair": 1 - group, "tm": place},
            device_id_type=MESH,
        )
        pair_copy.start()
        if it == 0:

            @pl.when(is_last)
            def _():
                wrap_copy.start()

        if it > 0:
            linear_part()
        v = value[...]
        cubic = react[...] * v
        pair_copy.wait()
        other = partner[it]

        @pl.when(group == 0)
        def _():
            rhs[...] -= cubic * v * v + GAMMA_INV * other

        @pl.when(group == 1)
        def _():
            rhs[...] -= 3.0 * cubic * other * other - other

        if it == 0:

            @pl.when(is_last)
            def _():
                wrap_copy.wait_send()

            @pl.when(is_first)
            def _():
                wrap_copy.wait_recv()
                rhs[...] -= alpha * wrapped[...]

        modes = dot_left(high[...], low[...], dot_right(rhs[...], high[...], low[...]))
        for m in range(STEPS):
            r, c = SUB * (m // 2), LANES * (m % 2)
            send[0, m] = modes[r : r + SUB, c : c + LANES]
        exchange(2 * it)
        exchange_wait(2 * it)

        def slot(i):
            return i + group * (STEPS - 1 - 2 * i)

        runs = STEPS // RUN
        state = [jnp.zeros_like(ratio) for _ in range(runs)]
        for j in range(RUN):
            for b in range(runs):
                n = slot(b * RUN + j)
                state[b] = ratio * (state[b] + recv[2 * it, n])
                send[1, n] = state[b]
        ends = [state[0]]
        for b in range(1, runs):
            ends.append(state[b] + run_power * ends[-1])
        carry = wrap_gain * (ends[-1] - last)
        last = ends[-1] + full_power * carry
        carries = [carry]
        for b in range(1, runs):
            carry = run_power * carry
            carries.append(ends[b - 1] + carry)
        for j in range(RUN):
            for b in range(runs):
                n = slot(b * RUN + j)
                carries[b] = ratio * carries[b]
                send[1, n] += carries[b]
        exchange(2 * it + 1)
        exchange_wait(2 * it + 1)
        for r in range(SIZE // 8):
            for c in range(SIZE // LANES):
                grid[8 * r : 8 * r + 8, LANES * c : LANES * c + LANES] = jnp.concatenate(
                    [recv[2 * it + 1, 4 * r + c], recv[2 * it + 1, 4 * r + 2 + c]], 0
                )
        result = dot_left(high[...], low[...], dot_right(grid[...], high[...], low[...]))
        if it == ITERS - 1:
            out[...] = result
        else:
            value[...] = result


def on_device(fields, forcing, diffusion, reaction, wrap_factor, mean_diffusion, spectral_shift):
    high, low, eigen = constants()
    any_space = pl.BlockSpec(memory_space=pl.ANY)
    scalar = pl.BlockSpec(memory_space=pltpu.SMEM)
    full = (SIZE, SIZE)
    block = (STEPS, SUB, LANES)
    result = pl.pallas_call(
        kernel,
        out_shape=jax.ShapeDtypeStruct(full, jnp.float32),
        in_specs=[any_space] * 4 + [scalar] * 3 + [any_space] * 3,
        out_specs=pl.BlockSpec(memory_space=pltpu.VMEM),
        scratch_shapes=[
            pltpu.VMEM(full, jnp.float32),
            pltpu.VMEM(full, jnp.float32),
            pltpu.VMEM(full, jnp.float32),
            pltpu.VMEM(full, jnp.float32),
            pltpu.VMEM(full, jnp.bfloat16),
            pltpu.VMEM(full, jnp.bfloat16),
            pltpu.VMEM((SUB, LANES), jnp.float32),
            pltpu.VMEM((ITERS,) + full, jnp.float32),
            pltpu.VMEM(full, jnp.float32),
            pltpu.VMEM(full, jnp.float32),
            pltpu.VMEM((5,) + full, jnp.float32),
            pltpu.VMEM(full, jnp.float32),
            pltpu.VMEM((2,) + block, jnp.float32),
            pltpu.VMEM((2 * ITERS,) + block, jnp.float32),
            pltpu.SemaphoreType.DMA((7,)),
            pltpu.SemaphoreType.DMA((ITERS,)),
            pltpu.SemaphoreType.DMA((ITERS,)),
            pltpu.SemaphoreType.DMA((2,)),
            pltpu.SemaphoreType.DMA((2 * ITERS,)),
            pltpu.SemaphoreType.DMA((2 * ITERS,)),
        ],
        compiler_params=pltpu.CompilerParams(
            collective_id=0, has_side_effects=True, vmem_limit_bytes=48 * 1024 * 1024
        ),
    )(
        fields.reshape(full), forcing.reshape(full), diffusion, reaction,
        wrap_factor, mean_diffusion, spectral_shift, high, low, eigen,
    )
    return result[None, None]


def solution(mesh):
    split = P("pair", "tm", None, None)
    return jax.shard_map(
        on_device,
        mesh=mesh,
        in_specs=(split, split, P(), P(), P(), P(), P()),
        out_specs=split,
        check_vma=False,
    )
```

time: 116 us -> 80.4 us (0.69)
  Pallas kernels: 0 us -> 70.8 us
  blocking collectives: 58.6 us -> 0 us
  starting transfers between devices: 23.6 us -> 0 us
  waiting for transfers between devices: 19.3 us -> 0 us
  matrix products: 3.25 us -> 0 us
  other arithmetic: 2.98 us -> 0 us
  local copies, waits for them, and re-layouts: 5.14 us -> 7.25 us
    pallas_call x0 -> x1, Pallas kernels: none -> 70.8 us  [on_device(): pl.pallas_call(kernel, out_shape=jax.ShapeDtypeStruct(full, jnp.float32),...]
    all_to_all x3 -> x0, blocking collectives: 58.6 us -> none  [the longest x2 38.9 us: on_device(): modes = lax.all_to_all(times, 'tm', split_axis=0, concat_axis=0, tiled=True)]
    all_to_all x1 -> x0, starting transfers between devices: 15.4 us -> none  [on_device(): times = lax.all_to_all(modes, 'tm', split_axis=0, concat_axis=0, tiled=True)]
    all_to_all x1 -> x0, waiting for transfers between devices: 13.4 us -> none  [on_device(): times = lax.all_to_all(modes, 'tm', split_axis=0, concat_axis=0, tiled=True)]
    ppermute x3 -> x0, starting transfers between devices: 8.23 us -> none  [the longest x2 7.57 us: on_device(): partner = lax.ppermute(values, 'pair', [(0, 1), (1, 0)])]
    unnamed x14 -> x15, local copies, waits for them, and re-layouts: 0.99 us -> 7.25 us
    ppermute x3 -> x0, waiting for transfers between devices: 5.9 us -> none  [the longest x2 5.9 us: on_device(): partner = lax.ppermute(values, 'pair', [(0, 1), (1, 0)])]
    dot_general x8 -> x0, matrix products: 3.25 us -> none  [the longest x4 1.78 us: both_sides(): return jnp.dot(matrix, left, precision=lax.Precision.HIGH)]
  transfers between devices with their start and end apart: 4 -> 0, of which waited for: 2 -> 0; matrix products, arithmetic and copies ran while one was open for 2% -> 0% of each run, Pallas kernels for 0% -> 0%
where the time goes in v1:
time: 80.4 us; the launch traced here: 80.1 us
  Pallas kernels  70.8 us (88%)
  local copies, waits for them, and re-layouts  7.25 us (9%)
  between operations  1.96 us (2%)
    pallas_call x1, Pallas kernels, on_device(): pl.pallas_call(kernel, out_shape=jax.ShapeDtypeStruct(full, jnp.float32),...  70.8 us
    unnamed x15, local copies, waits for them, and re-layouts  7.25 us

profile of v1, /device:TPU:1, one launch (start us, length us, event | category | flops | bytes accessed | tf_op | source)
XLA Modules:
  0.0 80.1 jit_solution(16956411157606953298)
XLA Ops:
  1.9 0.0 copy-start
  2.0 0.9 %copy-done = f32[1,1,256,256]{3,2,1,0:T(8,128)S(1)} copy-done((f32[1,1,256,256]{3,2,1,0:T(8,128)S(1)}, f32[1,1,256,256]{3,2,1,0:T(8,128)}, u32[]{:S(2)}) %copy-start) | copy-done | bytes 262168
  2.9 0.0 copy-start.1
  2.9 0.9 %copy-done.1 = f32[1,1,256,256]{3,2,1,0:T(8,128)S(1)} copy-done((f32[1,1,256,256]{3,2,1,0:T(8,128)S(1)}, f32[1,1,256,256]{3,2,1,0:T(8,128)}, u32[]{:S(2)}) %copy-start.1) | copy-done | bytes 262168
  3.8 0.0 copy-start.2
  3.8 0.9 %copy-done.2 = f32[256,256]{1,0:T(8,128)S(1)} copy-done((f32[256,256]{1,0:T(8,128)S(1)}, f32[256,256]{1,0:T(8,128)}, u32[]{:S(2)}) %copy-start.2) | copy-done | bytes 262168
  4.8 0.0 copy-start.3
  4.8 0.9 %copy-done.3 = f32[256,256]{1,0:T(8,128)S(1)} copy-done((f32[256,256]{1,0:T(8,128)S(1)}, f32[256,256]{1,0:T(8,128)}, u32[]{:S(2)}) %copy-start.3) | copy-done | bytes 262168
  5.7 0.0 copy-start.4
  5.7 0.9 %copy-done.4 = f32[128,4,128]{2,1,0:T(4,128)S(1)} copy-done((f32[128,4,128]{2,1,0:T(4,128)S(1)}, f32[128,4,128]{2,1,0:T(4,128)}, u32[]{:S(2)}) %copy-start.4) | copy-done | bytes 262168
  6.7 0.0 copy-start.5
  6.7 0.9 %copy-done.5 = bf16[256,256]{1,0:T(8,128)(2,1)S(1)} copy-done((bf16[256,256]{1,0:T(8,128)(2,1)S(1)}, bf16[256,256]{1,0:T(8,128)(2,1)}, u32[]{:S(2)}) %copy-start.5) | copy-done | bytes 131096
  7.6 0.0 copy-start.6
  7.6 0.9 %copy-done.6 = bf16[256,256]{1,0:T(8,128)(2,1)S(1)} copy-done((bf16[256,256]{1,0:T(8,128)(2,1)S(1)}, bf16[256,256]{1,0:T(8,128)(2,1)}, u32[]{:S(2)}) %copy-start.6) | copy-done | bytes 131096
  8.5 70.8 %shard_map.91 = f32[256,256]{1,0:T(8,128)S(1)} custom-call(f32[256,256]{1,0:T(8,128)S(1)} %bitcast.4, f32[256,256]{1,0:T(8,128)S(1)} %bitcast.5, f32[256,256]{1,0:T(8,128)S(1)} %copy-done.2, f32[256,256]{1,0:T(8,128)S(1)} %copy-done.3, f32[1]{0:T(128)S(6)} %copy.11.alpha_ref, f32[1]{0:T(128)S(6)} %copy.12.mean_ref, f32[1]{0:T(128)S(6)} %copy.13.shift_ref, ...), custom_call_target="tpu_custom_call" | custom-call | tf_op jit(solution)/shard_map/pallas_call | solution.py:247
  79.4 0.7 copy.14
Async XLA Ops:
  1.9 1.0 %copy-start = (f32[1,1,256,256]{3,2,1,0:T(8,128)S(1)}, f32[1,1,256,256]{3,2,1,0:T(8,128)}, u32[]{:S(2)}) copy-start(f32[1,1,256,256]{3,2,1,0:T(8,128)} %param.9) | copy-start | bytes 786436
  2.9 0.9 %copy-start.1 = (f32[1,1,256,256]{3,2,1,0:T(8,128)S(1)}, f32[1,1,256,256]{3,2,1,0:T(8,128)}, u32[]{:S(2)}) copy-start(f32[1,1,256,256]{3,2,1,0:T(8,128)} %param.10) | copy-start | bytes 786436
  3.8 0.9 %copy-start.2 = (f32[256,256]{1,0:T(8,128)S(1)}, f32[256,256]{1,0:T(8,128)}, u32[]{:S(2)}) copy-start(f32[256,256]{1,0:T(8,128)} %diffusion.1) | copy-start | bytes 786436
  4.8 0.9 %copy-start.3 = (f32[256,256]{1,0:T(8,128)S(1)}, f32[256,256]{1,0:T(8,128)}, u32[]{:S(2)}) copy-start(f32[256,256]{1,0:T(8,128)} %reaction.1) | copy-start | bytes 786436
  5.7 0.9 %copy-start.4 = (f32[128,4,128]{2,1,0:T(4,128)S(1)}, f32[128,4,128]{2,1,0:T(4,128)}, u32[]{:S(2)}) copy-start(f32[128,4,128]{2,1,0:T(4,128)} %constant.5.clone.eigen) | copy-start | bytes 786436
  6.7 0.9 %copy-start.5 = (bf16[256,256]{1,0:T(8,128)(2,1)S(1)}, bf16[256,256]{1,0:T(8,128)(2,1)}, u32[]{:S(2)}) copy-start(bf16[256,256]{1,0:T(8,128)(2,1)} %constant.11.low_in) | copy-start | bytes 393220
  7.6 0.9 %copy-start.6 = (bf16[256,256]{1,0:T(8,128)(2,1)S(1)}, bf16[256,256]{1,0:T(8,128)(2,1)}, u32[]{:S(2)}) copy-start(bf16[256,256]{1,0:T(8,128)(2,1)} %constant.8.high_in) | copy-start | bytes 393220

commit v2 on v1

--- a/solution.py
+++ b/solution.py
@@ -12,9 +12,11 @@
 GAMMA_INV = 0.5
 SIZE = 256
 STEPS = 128
+CHIPS = 64
+HALF = 128
 SUB = 4
 LANES = 128
-RUN = 16
+RUN = 8
 MESH = pl.DeviceIdType.MESH
 
 
@@ -30,8 +32,8 @@
     low = (matrix - high.astype(jnp.float32)).astype(jnp.bfloat16)
     sines = 4.0 * np.sin(np.arange(SIZE) * (math.pi / SIZE)) ** 2
     eigen = (sines[:, None] + sines[None, :]).astype(np.float32)
-    eigen = eigen.reshape(SIZE // SUB, SUB, SIZE // LANES, LANES).transpose(0, 2, 1, 3)
-    return high, low, jnp.asarray(eigen.reshape(STEPS, SUB, LANES))
+    bands = eigen.reshape(SIZE // SUB, SUB, SIZE // LANES, LANES).transpose(0, 2, 1, 3)
+    return high, low, jnp.asarray(eigen), jnp.asarray(bands.reshape(2 * CHIPS, SUB, LANES))
 
 
 def halves(values):
@@ -55,36 +57,45 @@
 
 def kernel(
     fields, forcing, diffusion, reaction, alpha_ref, mean_ref, shift_ref, high_in, low_in, eigen,
-    out, value, source, diff, react, high, low, eig, partner, wrapped, rhs,
-    coef, grid, send, recv, in_sems, pair_send, pair_recv, wrap_sems, all_send, all_recv,
+    bands, out, value, source, diff, react, high, low, eig, ratio_half, partner, wrapped, rhs,
+    coef, modes, swap, full, send, recv, in_sems, pair_send, pair_recv, wrap_sems, swap_send,
+    swap_recv, all_send, all_recv,
 ):
     group = lax.axis_index("pair")
     place = lax.axis_index("tm")
+    chip = place // 2
+    core = place % 2
     loads = [
         pltpu.make_async_copy(src, dst, in_sems.at[i])
         for i, (src, dst) in enumerate(
             (
                 (fields, value), (diffusion, diff), (forcing, source), (reaction, react),
-                (high_in, high), (low_in, low), (eigen.at[place], eig),
+                (high_in, high), (low_in, low), (bands.at[core * CHIPS + chip], eig),
+                (eigen.at[pl.ds(pl.multiple_of(core * HALF, HALF), HALF)], ratio_half),
             )
         )
     ]
     for load in loads:
         load.start()
 
+    is_first = place == (STEPS - 1) * group
+    is_last = place == (STEPS - 1) * (1 - group)
+    is_edge = (place == 0) | (place == STEPS - 1)
     barrier = pltpu.get_barrier_semaphore()
 
-    def greet(d, c):
+    def greet(pair, tm):
         pl.semaphore_signal(
-            barrier, inc=1, device_id={"pair": group, "tm": place ^ (STEPS - d)},
-            device_id_type=MESH,
-        )
-        return c
-
-    pl.semaphore_signal(
-        barrier, inc=1, device_id={"pair": 1 - group, "tm": place}, device_id_type=MESH
-    )
-    lax.fori_loop(1, STEPS, greet, 0)
+            barrier, inc=1, device_id={"pair": pair, "tm": tm}, device_id_type=MESH
+        )
+
+    @pl.when(is_edge)
+    def _():
+        greet(group, STEPS - 1 - place)
+
+    for d in range(CHIPS - 1, 0, -1):
+        greet(group, place ^ (2 * d))
+    greet(1 - group, place)
+    greet(group, place ^ 1)
 
     alpha = alpha_ref[0]
     mean = mean_ref[0]
@@ -110,49 +121,57 @@
         total += coef[2] * pltpu.roll(v, SIZE - 1, 1) + coef[3] * pltpu.roll(v, 1, 1)
         rhs[...] = total
 
-    lam = 1.0 + mean * eig[...] + shift
-    ratio = 1.0 / lam
-    run_power = ratio
-    for _ in range(4):
+    ratio_half[...] = 1.0 / (1.0 + mean * ratio_half[...] + shift)
+    ratio = 1.0 / (1.0 + mean * eig[...] + shift)
+    pair_ratio = ratio * ratio
+    run_power = pair_ratio
+    for _ in range(3):
         run_power = run_power * run_power
     full_power = run_power
     for _ in range(3):
         full_power = full_power * full_power
     wrap_gain = alpha / (1.0 - alpha * full_power)
     last = jnp.zeros_like(ratio)
+    own_rows = pl.ds(pl.multiple_of(core * HALF, HALF), HALF)
+    other_rows = pl.ds(pl.multiple_of((1 - core) * HALF, HALF), HALF)
+    own_first = core == group
 
     linear_part()
-    pl.semaphore_wait(barrier, STEPS)
-
-    is_first = place == (STEPS - 1) * group
-    is_last = place == (STEPS - 1) * (1 - group)
+    pl.semaphore_wait(barrier, CHIPS + 1 + is_edge.astype(jnp.int32))
+
     wrap_copy = pltpu.make_async_remote_copy(
         src_ref=value, dst_ref=wrapped, send_sem=wrap_sems.at[0], recv_sem=wrap_sems.at[1],
         device_id={"pair": group, "tm": STEPS - 1 - place}, device_id_type=MESH,
     )
 
     def exchange(phase):
-        def one(d, c):
-            peer = place ^ (STEPS - d)
+        for d in range(CHIPS - 1, 0, -1):
+            peer = chip ^ d
             pltpu.make_async_remote_copy(
-                src_ref=send.at[phase % 2, peer], dst_ref=recv.at[phase, place],
+                src_ref=send.at[phase % 2, peer], dst_ref=recv.at[phase, chip],
                 send_sem=all_send.at[phase], recv_sem=all_recv.at[phase],
-                device_id={"pair": group, "tm": peer}, device_id_type=MESH,
+                device_id={"pair": group, "tm": 2 * peer + core}, device_id_type=MESH,
             ).start()
-            return c
-
-        lax.fori_loop(1, STEPS, one, 0)
-        recv[phase, place] = send[phase % 2, place]
+        recv[phase, chip] = send[phase % 2, chip]
 
     def exchange_wait(phase):
-        span = pl.ds(0, STEPS - 1)
+        span = pl.ds(0, CHIPS - 1)
         wait = pltpu.make_async_remote_copy(
             src_ref=send.at[phase % 2, span], dst_ref=recv.at[phase, span],
             send_sem=all_send.at[phase], recv_sem=all_recv.at[phase],
-            device_id={"pair": group, "tm": place}, device_id_type=MESH,
+            device_id={"pair": group, "tm": place ^ 1}, device_id_type=MESH,
         )
         wait.wait_send()
         wait.wait_recv()
+
+    def swap_copy(index, src, dst):
+        return pltpu.make_async_remote_copy(
+            src_ref=src, dst_ref=dst, send_sem=swap_send.at[index], recv_sem=swap_recv.at[index],
+            device_id={"pair": group, "tm": place ^ 1}, device_id_type=MESH,
+        )
+
+    def slot(i):
+        return i + group * (CHIPS - 1 - 2 * i)
 
     for it in range(ITERS):
         pair_copy = pltpu.make_async_remote_copy(
@@ -193,23 +212,28 @@
                 wrap_copy.wait_recv()
                 rhs[...] -= alpha * wrapped[...]
 
-        modes = dot_left(high[...], low[...], dot_right(rhs[...], high[...], low[...]))
-        for m in range(STEPS):
+        modes[...] = dot_left(high[...], low[...], dot_right(rhs[...], high[...], low[...]))
+        there = swap_copy(2 * it, modes.at[other_rows], swap.at[2 * it])
+        there.start()
+        there.wait()
+        own, sibling = modes[own_rows], swap[2 * it]
+        q = ratio_half[...]
+        first = jnp.where(own_first, own, sibling)
+        second = jnp.where(own_first, sibling, own)
+        joined = q * (q * first + second)
+        for m in range(CHIPS):
             r, c = SUB * (m // 2), LANES * (m % 2)
-            send[0, m] = modes[r : r + SUB, c : c + LANES]
+            send[0, m] = joined[r : r + SUB, c : c + LANES]
         exchange(2 * it)
         exchange_wait(2 * it)
 
-        def slot(i):
-            return i + group * (STEPS - 1 - 2 * i)
-
-        runs = STEPS // RUN
+        runs = CHIPS // RUN
         state = [jnp.zeros_like(ratio) for _ in range(runs)]
         for j in range(RUN):
             for b in range(runs):
                 n = slot(b * RUN + j)
-                state[b] = ratio * (state[b] + recv[2 * it, n])
                 send[1, n] = state[b]
+                state[b] = pair_ratio * state[b] + recv[2 * it, n]
         ends = [state[0]]
         for b in range(1, runs):
             ends.append(state[b] + run_power * ends[-1])
@@ -222,16 +246,29 @@
         for j in range(RUN):
             for b in range(runs):
                 n = slot(b * RUN + j)
-                carries[b] = ratio * carries[b]
                 send[1, n] += carries[b]
+                carries[b] = pair_ratio * carries[b]
         exchange(2 * it + 1)
         exchange_wait(2 * it + 1)
-        for r in range(SIZE // 8):
-            for c in range(SIZE // LANES):
-                grid[8 * r : 8 * r + 8, LANES * c : LANES * c + LANES] = jnp.concatenate(
+        rows = []
+        for r in range(HALF // 8):
+            parts = [
+                jnp.concatenate(
                     [recv[2 * it + 1, 4 * r + c], recv[2 * it + 1, 4 * r + 2 + c]], 0
                 )
-        result = dot_left(high[...], low[...], dot_right(grid[...], high[...], low[...]))
+                for c in range(SIZE // LANES)
+            ]
+            rows.append(jnp.concatenate(parts, 1))
+        carry_in = jnp.concatenate(rows, 0)
+        own, sibling = modes[own_rows], swap[2 * it]
+        first = q * (carry_in + jnp.where(own_first, own, sibling))
+        second = q * (first + jnp.where(own_first, sibling, own))
+        full[it, own_rows] = jnp.where(own_first, first, second)
+        swap[2 * it + 1] = jnp.where(own_first, second, first)
+        back = swap_copy(2 * it + 1, swap.at[2 * it + 1], full.at[it, own_rows])
+        back.start()
+        back.wait()
+        result = dot_left(high[...], low[...], dot_right(full[it], high[...], low[...]))
         if it == ITERS - 1:
             out[...] = result
         else:
@@ -239,15 +276,16 @@
 
 
 def on_device(fields, forcing, diffusion, reaction, wrap_factor, mean_diffusion, spectral_shift):
-    high, low, eigen = constants()
+    high, low, eigen, bands = constants()
     any_space = pl.BlockSpec(memory_space=pl.ANY)
     scalar = pl.BlockSpec(memory_space=pltpu.SMEM)
     full = (SIZE, SIZE)
-    block = (STEPS, SUB, LANES)
+    half = (HALF, SIZE)
+    block = (CHIPS, SUB, LANES)
     result = pl.pallas_call(
         kernel,
         out_shape=jax.ShapeDtypeStruct(full, jnp.float32),
-        in_specs=[any_space] * 4 + [scalar] * 3 + [any_space] * 3,
+        in_specs=[any_space] * 4 + [scalar] * 3 + [any_space] * 4,
         out_specs=pl.BlockSpec(memory_space=pltpu.VMEM),
         scratch_shapes=[
             pltpu.VMEM(full, jnp.float32),
@@ -257,26 +295,31 @@
             pltpu.VMEM(full, jnp.bfloat16),
             pltpu.VMEM(full, jnp.bfloat16),
             pltpu.VMEM((SUB, LANES), jnp.float32),
+            pltpu.VMEM(half, jnp.float32),
             pltpu.VMEM((ITERS,) + full, jnp.float32),
             pltpu.VMEM(full, jnp.float32),
             pltpu.VMEM(full, jnp.float32),
             pltpu.VMEM((5,) + full, jnp.float32),
             pltpu.VMEM(full, jnp.float32),
+            pltpu.VMEM((2 * ITERS,) + half, jnp.float32),
+            pltpu.VMEM((ITERS,) + full, jnp.float32),
             pltpu.VMEM((2,) + block, jnp.float32),
             pltpu.VMEM((2 * ITERS,) + block, jnp.float32),
-            pltpu.SemaphoreType.DMA((7,)),
+            pltpu.SemaphoreType.DMA((8,)),
             pltpu.SemaphoreType.DMA((ITERS,)),
             pltpu.SemaphoreType.DMA((ITERS,)),
             pltpu.SemaphoreType.DMA((2,)),
             pltpu.SemaphoreType.DMA((2 * ITERS,)),
             pltpu.SemaphoreType.DMA((2 * ITERS,)),
+            pltpu.SemaphoreType.DMA((2 * ITERS,)),
+            pltpu.SemaphoreType.DMA((2 * ITERS,)),
         ],
         compiler_params=pltpu.CompilerParams(
-            collective_id=0, has_side_effects=True, vmem_limit_bytes=48 * 1024 * 1024
+            collective_id=0, has_side_effects=True, vmem_limit_bytes=67043328
         ),
     )(
         fields.reshape(full), forcing.reshape(full), diffusion, reaction,
-        wrap_factor, mean_diffusion, spectral_shift, high, low, eigen,
+        wrap_factor, mean_diffusion, spectral_shift, high, low, eigen, bands,
     )
     return result[None, None]
 

time: 80.4 us -> 70.7 us (0.88)
  local copies, waits for them, and re-layouts: 7.25 us -> 1.67 us
  Pallas kernels: 70.8 us -> 66.9 us
    unnamed x15 -> x1, local copies, waits for them, and re-layouts: 7.25 us -> 1.67 us
    pallas_call x1, Pallas kernels: 70.8 us -> 66.9 us  [on_device(): pl.pallas_call(kernel, out_shape=jax.ShapeDtypeStruct(full, jnp.float32),...]
where the time goes in v2:
time: 70.7 us; the launch traced here: 70.5 us
  Pallas kernels  66.9 us (95%)
  between operations  1.95 us (3%)
  local copies, waits for them, and re-layouts  1.67 us (2%)
    pallas_call x1, Pallas kernels, on_device(): pl.pallas_call(kernel, out_shape=jax.ShapeDtypeStruct(full, jnp.float32),...  66.9 us
    unnamed x1, local copies, waits for them, and re-layouts  1.67 us

profile of v2, /device:TPU:1, one launch (start us, length us, event | category | flops | bytes accessed | tf_op | source)
XLA Modules:
  0.0 70.5 jit_solution(4901038228444485450)
XLA Ops:
  1.9 66.9 %shard_map.100 = f32[256,256]{1,0:T(8,128)} custom-call(f32[256,256]{1,0:T(8,128)} %bitcast.4, f32[256,256]{1,0:T(8,128)} %bitcast.5, f32[256,256]{1,0:T(8,128)} %diffusion.1, f32[256,256]{1,0:T(8,128)} %reaction.1, f32[1]{0:T(128)S(6)} %copy.12.alpha_ref, f32[1]{0:T(128)S(6)} %copy.13.mean_ref, f32[1]{0:T(128)S(6)} %copy.14.shift_ref, ...), custom_call_target="tpu_custom_call" | custom-call | tf_op jit(solution)/shard_map/pallas_call | solution.py:285
  68.9 1.7 %copy.15 = f32[1,1,256,256]{3,2,1,0:T(8,128)} copy(f32[1,1,256,256]{3,2,1,0:T(8,128)} %bitcast.3) | data formatting | bytes 524288

commit v3 on v2

v3 whole, which is shorter than its diff:
```python
import math

import jax
import jax.numpy as jnp
import numpy as np
from jax import lax
from jax.experimental import pallas as pl
from jax.experimental.pallas import tpu as pltpu
from jax.sharding import PartitionSpec as P

ITERS = 2
GAMMA_INV = 0.5
SIZE = 256
STEPS = 128
CHIPS = 64
HALF = 128
SUB = 4
LANES = 128
RUN = 8
MESH = pl.DeviceIdType.MESH


def cas_matrix(length):
    wrapped = np.outer(np.arange(length), np.arange(length)) % length
    angles = wrapped * (2.0 * math.pi / length)
    return (np.cos(angles) + np.sin(angles)) / math.sqrt(length)


def constants():
    matrix = jnp.asarray(cas_matrix(SIZE), jnp.float32)
    high = matrix.astype(jnp.bfloat16)
    low = (matrix - high.astype(jnp.float32)).astype(jnp.bfloat16)
    sines = 4.0 * np.sin(np.arange(SIZE) * (math.pi / SIZE)) ** 2
    eigen = (sines[:, None] + sines[None, :]).astype(np.float32)
    bands = eigen.reshape(SIZE // SUB, SUB, SIZE // LANES, LANES).transpose(0, 2, 1, 3)
    return high, low, jnp.asarray(eigen), jnp.asarray(bands.reshape(2 * CHIPS, SUB, LANES))


def halves(values):
    high = values.astype(jnp.bfloat16)
    return high, (values - high.astype(jnp.float32)).astype(jnp.bfloat16)


def dot(a, b):
    return jnp.dot(a, b, preferred_element_type=jnp.float32)


def dot_right(values, high, low):
    vh, vl = halves(values)
    return dot(vh, high) + (dot(vl, high) + dot(vh, low))


def dot_left(high, low, values):
    vh, vl = halves(values)
    return dot(high, vh) + (dot(high, vl) + dot(low, vh))


def kernel(
    fields, forcing, diffusion, reaction, wrap_in, mean_in, shift_in, high_in, low_in, eigen,
    bands, out, wrap_ref, mean_ref, shift_ref, value, source, diff, react, high, low, eig, ratio,
    gain, partner, wrapped, rhs, coef, modes, sibling, part, part_far, joined, arrived, give,
    carry, in_sems, pair_sems, wrap_sems, part_sems, local_sems, swap_send, swap_recv, out_send,
    out_recv, back_send, back_recv, met,
):
    group = lax.axis_index("pair")
    place = lax.axis_index("tm")
    chip = place // 2
    core = place % 2
    loads = [
        pltpu.make_async_copy(src, dst, in_sems.at[i])
        for i, (src, dst) in enumerate(
            (
                (fields, value), (diffusion, diff), (wrap_in, wrap_ref), (mean_in, mean_ref),
                (shift_in, shift_ref), (forcing, source), (eigen, ratio),
                (bands.at[core * CHIPS + chip], eig), (reaction, react), (high_in, high),
                (low_in, low),
            )
        )
    ]
    for load in loads:
        load.start()

    is_first = place == (STEPS - 1) * group
    is_last = place == (STEPS - 1) * (1 - group)
    is_edge = (place == 0) | (place == STEPS - 1)
    barrier = pltpu.get_barrier_semaphore()

    def greet(pair, tm):
        pl.semaphore_signal(
            barrier, inc=1, device_id={"pair": pair, "tm": tm}, device_id_type=MESH
        )

    @pl.when(is_edge)
    def _():
        greet(group, STEPS - 1 - place)

    def chip_at(move_y, move_x, move_z):
        y = (chip // 32 + move_y) % 2
        x = (chip // 8 + move_x) % 4
        z = (chip + move_z) % 8
        return 2 * (32 * y + 8 * x + z) + core

    along_z = [chip_at(0, 0, move) for move in (1, 7, 2, 6)]
    along_x = [chip_at(0, move, 0) for move in (1, 2, 3)]
    along_y = [chip_at(1, 0, 0)]
    greet(1 - group, place)
    for tm in along_z + along_x + along_y + [place ^ 1]:
        greet(group, tm)
    pl.semaphore_wait(barrier, 10 + is_edge.astype(jnp.int32))

    def remote(src, dst, send_sem, recv_sem, pair, tm):
        return pltpu.make_async_remote_copy(
            src_ref=src, dst_ref=dst, send_sem=send_sem, recv_sem=recv_sem,
            device_id={"pair": pair, "tm": tm}, device_id_type=MESH,
        )

    pair_copy = remote(fields, partner, pair_sems.at[0], pair_sems.at[1], 1 - group, place)
    wrap_copy = remote(
        fields, wrapped, wrap_sems.at[0], wrap_sems.at[1], group, STEPS - 1 - place
    )
    pair_copy.start()

    @pl.when(is_last)
    def _():
        wrap_copy.start()

    for load in loads:
        load.wait()

    for stage, peers in enumerate((along_z, along_x, along_y)):
        for tm in peers:
            pl.semaphore_signal(
                met.at[stage], inc=1, device_id={"pair": group, "tm": tm}, device_id_type=MESH
            )
        pl.semaphore_wait(met.at[stage], len(peers))

    alpha = wrap_ref[0]
    mean = mean_ref[0]
    shift = shift_ref[0]

    d = diff[...]
    east = 0.5 * (d + pltpu.roll(d, SIZE - 1, 0)) - mean
    north = 0.5 * (d + pltpu.roll(d, SIZE - 1, 1)) - mean
    west = pltpu.roll(east, 1, 0)
    south = pltpu.roll(north, 1, 1)
    coef[0] = east
    coef[1] = west
    coef[2] = north
    coef[3] = south
    coef[4] = shift - ((east + west) + (north + south))

    def linear_part():
        v = value[...]
        total = source[...] + coef[4] * v
        total += coef[0] * pltpu.roll(v, SIZE - 1, 0) + coef[1] * pltpu.roll(v, 1, 0)
        total += coef[2] * pltpu.roll(v, SIZE - 1, 1) + coef[3] * pltpu.roll(v, 1, 1)
        rhs[...] = total

    own_first = core == group
    single = 1.0 / (1.0 + mean * ratio[...] + shift)
    ratio[...] = single
    gain[0] = jnp.where(own_first, single, single * single)
    gain[1] = jnp.where(own_first, single * single, single)
    band_ratio = 1.0 / (1.0 + mean * eig[...] + shift)
    pair_ratio = band_ratio * band_ratio
    run_power = pair_ratio
    for _ in range(3):
        run_power = run_power * run_power
    full_power = run_power
    for _ in range(3):
        full_power = full_power * full_power
    wrap_gain = alpha / (1.0 - alpha * full_power)
    last = jnp.zeros_like(band_ratio)
    own_rows = pl.ds(pl.multiple_of(core * HALF, HALF), HALF)

    def band(k, offset):
        rows = pl.ds(pl.multiple_of(offset + SUB * (k // 2), SUB), SUB)
        return rows, pl.ds(pl.multiple_of(LANES * (k % 2), LANES), LANES)

    my_rows, my_lanes = band(chip, core * HALF)

    linear_part()

    def slot(i):
        return i + group * (CHIPS - 1 - 2 * i)

    def couple(other):
        v = value[...]
        cubic = react[...] * v

        @pl.when(group == 0)
        def _():
            rhs[...] -= cubic * v * v + GAMMA_INV * other

        @pl.when(group == 1)
        def _():
            rhs[...] -= 3.0 * cubic * other * other - other

    pair_copy.wait()
    couple(partner[...])

    @pl.when(is_last)
    def _():
        wrap_copy.wait_send()

    @pl.when(is_first)
    def _():
        wrap_copy.wait_recv()
        rhs[...] -= alpha * wrapped[...]

    part_copy = remote(part, part_far, part_sems.at[0], part_sems.at[1], 1 - group, place)

    for it in range(ITERS):
        final = it == ITERS - 1
        modes[it] = dot_left(high[...], low[...], dot_right(rhs[...], high[...], low[...]))
        swap = remote(
            modes.at[it], sibling.at[it], swap_send.at[it, 0], swap_recv.at[it, 0], group,
            place ^ 1,
        )
        swap.start()
        swap.wait()
        near, beside = modes[it, own_rows], sibling[it, own_rows]
        q = ratio[own_rows]
        joined[...] = q * jnp.where(own_first, q * near + beside, q * beside + near)
        for d in range(CHIPS - 1, 0, -1):
            peer = chip ^ d
            rows, lanes = band(peer, 0)
            remote(
                joined.at[rows, lanes], arrived.at[it, chip], out_send.at[it], out_recv.at[it],
                group, place ^ (2 * d),
            ).start()
        rows, lanes = band(chip, 0)
        keep = pltpu.make_async_copy(
            joined.at[rows, lanes], arrived.at[it, chip], local_sems.at[it, 0]
        )
        keep.start()
        near = modes[it]
        part[...] = ratio[...] * jnp.where(own_first, near, near + ratio[...] * sibling[it])
        keep.wait()
        span = pl.ds(0, CHIPS - 1)
        wait = remote(
            give.at[span], arrived.at[it, span], out_send.at[it], out_recv.at[it], group,
            place ^ 1,
        )
        wait.wait_send()
        wait.wait_recv()

        runs = CHIPS // RUN
        state = [jnp.zeros_like(band_ratio) for _ in range(runs)]
        for j in range(RUN):
            for b in range(runs):
                n = slot(b * RUN + j)
                give[n] = state[b]
                state[b] = pair_ratio * state[b] + arrived[it, n]
        ends = [state[0]]
        for b in range(1, runs):
            ends.append(state[b] + run_power * ends[-1])
        enter = wrap_gain * (ends[-1] - last)
        last = ends[-1] + full_power * enter
        enters = [enter]
        for b in range(1, runs):
            enter = run_power * enter
            enters.append(ends[b - 1] + enter)
        for j in range(RUN):
            for b in range(runs):
                n = slot(b * RUN + j)
                give[n] += enters[b]
                enters[b] = pair_ratio * enters[b]

        for d in range(CHIPS - 1, -1, -1):
            peer = chip ^ d
            if not final:
                remote(
                    give.at[peer], carry.at[it, 1, my_rows, my_lanes], back_send.at[it, 1],
                    back_recv.at[it, 1], 1 - group, place ^ (2 * d),
                ).start()
            if d:
                remote(
                    give.at[peer], carry.at[it, 0, my_rows, my_lanes], back_send.at[it, 0],
                    back_recv.at[it, 0], group, place ^ (2 * d),
                ).start()
        keep = pltpu.make_async_copy(
            give.at[chip], carry.at[it, 0, my_rows, my_lanes], local_sems.at[it, 1]
        )
        keep.start()
        keep.wait()
        if not final:
            part_copy.start()
        kinds = 1 if final else 2
        swaps = []
        for kind in range(kinds):
            count = CHIPS - 1 + kind
            wait = remote(
                give.at[pl.ds(0, count)], arrived.at[it, pl.ds(0, count)],
                back_send.at[it, kind], back_recv.at[it, kind], group, place ^ 1,
            )
            wait.wait_send()
            wait.wait_recv()
            swap = remote(
                carry.at[it, kind, own_rows], carry.at[it, kind, own_rows],
                swap_send.at[it, 1 + kind], swap_recv.at[it, 1 + kind], group, place ^ 1,
            )
            swap.start()
            swaps.append(swap)
        swaps[0].wait()
        full = gain[0] * carry[it, 0] + part[...]
        result = dot_left(high[...], low[...], dot_right(full, high[...], low[...]))
        if final:
            out[...] = result
        else:
            value[...] = result
            linear_part()
            swaps[1].wait()
            part_copy.wait()
            full = gain[1] * carry[it, 1] + part_far[...]
            couple(dot_left(high[...], low[...], dot_right(full, high[...], low[...])))


def on_device(fields, forcing, diffusion, reaction, wrap_factor, mean_diffusion, spectral_shift):
    high, low, eigen, bands = constants()
    any_space = pl.BlockSpec(memory_space=pl.ANY)
    full = (SIZE, SIZE)
    half = (HALF, SIZE)
    block = (CHIPS, SUB, LANES)
    f32 = jnp.float32
    result = pl.pallas_call(
        kernel,
        out_shape=jax.ShapeDtypeStruct(full, f32),
        in_specs=[any_space] * 11,
        out_specs=pl.BlockSpec(memory_space=pltpu.VMEM),
        scratch_shapes=[
            pltpu.SMEM((1,), f32),
            pltpu.SMEM((1,), f32),
            pltpu.SMEM((1,), f32),
            pltpu.VMEM(full, f32),
            pltpu.VMEM(full, f32),
            pltpu.VMEM(full, f32),
            pltpu.VMEM(full, f32),
            pltpu.VMEM(full, jnp.bfloat16),
            pltpu.VMEM(full, jnp.bfloat16),
            pltpu.VMEM((SUB, LANES), f32),
            pltpu.VMEM(full, f32),
            pltpu.VMEM((2,) + full, f32),
            pltpu.VMEM(full, f32),
            pltpu.VMEM(full, f32),
            pltpu.VMEM(full, f32),
            pltpu.VMEM((5,) + full, f32),
            pltpu.VMEM((ITERS,) + full, f32),
            pltpu.VMEM((ITERS,) + full, f32),
            pltpu.VMEM(full, f32),
            pltpu.VMEM(full, f32),
            pltpu.VMEM(half, f32),
            pltpu.VMEM((ITERS,) + block, f32),
            pltpu.VMEM(block, f32),
            pltpu.VMEM((ITERS, 2) + full, f32),
            pltpu.SemaphoreType.DMA((11,)),
            pltpu.SemaphoreType.DMA((2,)),
            pltpu.SemaphoreType.DMA((2,)),
            pltpu.SemaphoreType.DMA((2,)),
            pltpu.SemaphoreType.DMA((ITERS, 2)),
            pltpu.SemaphoreType.DMA((ITERS, 3)),
            pltpu.SemaphoreType.DMA((ITERS, 3)),
            pltpu.SemaphoreType.DMA((ITERS,)),
            pltpu.SemaphoreType.DMA((ITERS,)),
            pltpu.SemaphoreType.DMA((ITERS, 2)),
            pltpu.SemaphoreType.DMA((ITERS, 2)),
            pltpu.SemaphoreType.REGULAR((3,)),
        ],
        compiler_params=pltpu.CompilerParams(
            collective_id=0, has_side_effects=True, vmem_limit_bytes=67043328
        ),
    )(
        fields.reshape(full), forcing.reshape(full), diffusion, reaction,
        wrap_factor, mean_diffusion, spectral_shift, high, low, eigen, bands,
    )
    return result[None, None]


def solution(mesh):
    split = P("pair", "tm", None, None)
    return jax.shard_map(
        on_device,
        mesh=mesh,
        in_specs=(split, split, P(), P(), P(), P(), P()),
        out_specs=split,
        check_vma=False,
    )
```

time: 70.7 us -> 63.1 us (0.89)
  Pallas kernels: 66.9 us -> 59.3 us
    pallas_call x1, Pallas kernels: 66.9 us -> 59.3 us  [on_device(): pl.pallas_call(kernel, out_shape=jax.ShapeDtypeStruct(full, f32), in_spec...]
where the time goes in v3:
time: 63.1 us; the launch traced here: 63 us
  Pallas kernels  59.3 us (94%)
  between operations  1.95 us (3%)
  local copies, waits for them, and re-layouts  1.67 us (3%)
    pallas_call x1, Pallas kernels, on_device(): pl.pallas_call(kernel, out_shape=jax.ShapeDtypeStruct(full, f32), in_spec...  59.3 us
    unnamed x1, local copies, waits for them, and re-layouts  1.67 us

profile of v3, /device:TPU:1, one launch (start us, length us, event | category | flops | bytes accessed | tf_op | source)
XLA Modules:
  0.0 63.0 jit_solution(10212622424609248573)
XLA Ops:
  1.9 59.3 %shard_map.100 = f32[256,256]{1,0:T(8,128)} custom-call(f32[256,256]{1,0:T(8,128)} %bitcast.4, f32[256,256]{1,0:T(8,128)} %bitcast.5, f32[256,256]{1,0:T(8,128)} %diffusion.1, f32[256,256]{1,0:T(8,128)} %reaction.1, f32[1]{0:T(128)S(6)} %copy.12.wrap_in, f32[1]{0:T(128)S(6)} %copy.13.mean_in, f32[1]{0:T(128)S(6)} %copy.14.shift_in, ...), custom_call_target="tpu_custom_call" | custom-call | tf_op jit(solution)/shard_map/pallas_call | solution.py:326
  61.3 1.7 %copy.15 = f32[1,1,256,256]{3,2,1,0:T(8,128)} copy(f32[1,1,256,256]{3,2,1,0:T(8,128)} %bitcast.3) | data formatting | bytes 524288

commit v4 on v3

--- a/solution.py
+++ b/solution.py
@@ -27,13 +27,9 @@
 
 
 def constants():
-    matrix = jnp.asarray(cas_matrix(SIZE), jnp.float32)
-    high = matrix.astype(jnp.bfloat16)
-    low = (matrix - high.astype(jnp.float32)).astype(jnp.bfloat16)
     sines = 4.0 * np.sin(np.arange(SIZE) * (math.pi / SIZE)) ** 2
-    eigen = (sines[:, None] + sines[None, :]).astype(np.float32)
-    bands = eigen.reshape(SIZE // SUB, SUB, SIZE // LANES, LANES).transpose(0, 2, 1, 3)
-    return high, low, jnp.asarray(eigen), jnp.asarray(bands.reshape(2 * CHIPS, SUB, LANES))
+    tables = np.concatenate([cas_matrix(SIZE), sines[:, None] + sines[None, :]])
+    return jnp.asarray(tables, jnp.float32)
 
 
 def halves(values):
@@ -56,8 +52,7 @@
 
 
 def kernel(
-    fields, forcing, diffusion, reaction, wrap_in, mean_in, shift_in, high_in, low_in, eigen,
-    bands, out, wrap_ref, mean_ref, shift_ref, value, source, diff, react, high, low, eig, ratio,
+    fields, forcing, diffusion, reaction, wrap_in, mean_in, shift_in, tables, out, wrap_ref, mean_ref, shift_ref, value, source, diff, react, matrix, high, low, eig, ratio,
     gain, partner, wrapped, rhs, coef, modes, sibling, part, part_far, joined, arrived, give,
     carry, in_sems, pair_sems, wrap_sems, part_sems, local_sems, swap_send, swap_recv, out_send,
     out_recv, back_send, back_recv, met,
@@ -66,14 +61,21 @@
     place = lax.axis_index("tm")
     chip = place // 2
     core = place % 2
+
+    def band(k, offset):
+        rows = pl.ds(pl.multiple_of(offset + SUB * (k // 2), SUB), SUB)
+        return rows, pl.ds(pl.multiple_of(LANES * (k % 2), LANES), LANES)
+
+    my_rows, my_lanes = band(chip, core * HALF)
+    my_eigen, _ = band(chip, SIZE + core * HALF)
     loads = [
         pltpu.make_async_copy(src, dst, in_sems.at[i])
         for i, (src, dst) in enumerate(
             (
                 (fields, value), (diffusion, diff), (wrap_in, wrap_ref), (mean_in, mean_ref),
-                (shift_in, shift_ref), (forcing, source), (eigen, ratio),
-                (bands.at[core * CHIPS + chip], eig), (reaction, react), (high_in, high),
-                (low_in, low),
+                (shift_in, shift_ref), (forcing, source),
+                (tables.at[pl.ds(SIZE, SIZE)], ratio), (tables.at[my_eigen, my_lanes], eig),
+                (reaction, react), (tables.at[pl.ds(0, SIZE)], matrix),
             )
         )
     ]
@@ -138,6 +140,7 @@
     mean = mean_ref[0]
     shift = shift_ref[0]
 
+    high[...], low[...] = halves(matrix[...])
     d = diff[...]
     east = 0.5 * (d + pltpu.roll(d, SIZE - 1, 0)) - mean
     north = 0.5 * (d + pltpu.roll(d, SIZE - 1, 1)) - mean
@@ -173,11 +176,8 @@
     last = jnp.zeros_like(band_ratio)
     own_rows = pl.ds(pl.multiple_of(core * HALF, HALF), HALF)
 
-    def band(k, offset):
-        rows = pl.ds(pl.multiple_of(offset + SUB * (k // 2), SUB), SUB)
-        return rows, pl.ds(pl.multiple_of(LANES * (k % 2), LANES), LANES)
-
-    my_rows, my_lanes = band(chip, core * HALF)
+    other_rows = pl.ds(pl.multiple_of((1 - core) * HALF, HALF), HALF)
+
 
     linear_part()
 
@@ -212,13 +212,18 @@
 
     for it in range(ITERS):
         final = it == ITERS - 1
-        modes[it] = dot_left(high[...], low[...], dot_right(rhs[...], high[...], low[...]))
-        swap = remote(
-            modes.at[it], sibling.at[it], swap_send.at[it, 0], swap_recv.at[it, 0], group,
-            place ^ 1,
-        )
-        swap.start()
-        swap.wait()
+        turned = dot_right(rhs[...], high[...], low[...])
+        swaps = []
+        for i, rows in enumerate((other_rows, own_rows)):
+            modes[it, rows] = dot_left(high[rows], low[rows], turned)
+            swaps.append(
+                remote(
+                    modes.at[it, rows], sibling.at[it, rows], swap_send.at[it, i],
+                    swap_recv.at[it, i], group, place ^ 1,
+                )
+            )
+            swaps[-1].start()
+        swaps[0].wait()
         near, beside = modes[it, own_rows], sibling[it, own_rows]
         q = ratio[own_rows]
         joined[...] = q * jnp.where(own_first, q * near + beside, q * beside + near)
@@ -234,6 +239,7 @@
             joined.at[rows, lanes], arrived.at[it, chip], local_sems.at[it, 0]
         )
         keep.start()
+        swaps[1].wait()
         near = modes[it]
         part[...] = ratio[...] * jnp.where(own_first, near, near + ratio[...] * sibling[it])
         keep.wait()
@@ -298,7 +304,7 @@
             wait.wait_recv()
             swap = remote(
                 carry.at[it, kind, own_rows], carry.at[it, kind, own_rows],
-                swap_send.at[it, 1 + kind], swap_recv.at[it, 1 + kind], group, place ^ 1,
+                swap_send.at[it, 2 + kind], swap_recv.at[it, 2 + kind], group, place ^ 1,
             )
             swap.start()
             swaps.append(swap)
@@ -317,7 +323,7 @@
 
 
 def on_device(fields, forcing, diffusion, reaction, wrap_factor, mean_diffusion, spectral_shift):
-    high, low, eigen, bands = constants()
+    tables = constants()
     any_space = pl.BlockSpec(memory_space=pl.ANY)
     full = (SIZE, SIZE)
     half = (HALF, SIZE)
@@ -326,7 +332,7 @@
     result = pl.pallas_call(
         kernel,
         out_shape=jax.ShapeDtypeStruct(full, f32),
-        in_specs=[any_space] * 11,
+        in_specs=[any_space] * 8,
         out_specs=pl.BlockSpec(memory_space=pltpu.VMEM),
         scratch_shapes=[
             pltpu.SMEM((1,), f32),
@@ -336,6 +342,7 @@
             pltpu.VMEM(full, f32),
             pltpu.VMEM(full, f32),
             pltpu.VMEM(full, f32),
+            pltpu.VMEM(full, f32),
             pltpu.VMEM(full, jnp.bfloat16),
             pltpu.VMEM(full, jnp.bfloat16),
             pltpu.VMEM((SUB, LANES), f32),
@@ -353,13 +360,13 @@
             pltpu.VMEM((ITERS,) + block, f32),
             pltpu.VMEM(block, f32),
             pltpu.VMEM((ITERS, 2) + full, f32),
-            pltpu.SemaphoreType.DMA((11,)),
+            pltpu.SemaphoreType.DMA((10,)),
             pltpu.SemaphoreType.DMA((2,)),
             pltpu.SemaphoreType.DMA((2,)),
             pltpu.SemaphoreType.DMA((2,)),
             pltpu.SemaphoreType.DMA((ITERS, 2)),
-            pltpu.SemaphoreType.DMA((ITERS, 3)),
-            pltpu.SemaphoreType.DMA((ITERS, 3)),
+            pltpu.SemaphoreType.DMA((ITERS, 4)),
+            pltpu.SemaphoreType.DMA((ITERS, 4)),
             pltpu.SemaphoreType.DMA((ITERS,)),
             pltpu.SemaphoreType.DMA((ITERS,)),
             pltpu.SemaphoreType.DMA((ITERS, 2)),
@@ -367,11 +374,11 @@
             pltpu.SemaphoreType.REGULAR((3,)),
         ],
         compiler_params=pltpu.CompilerParams(
-            collective_id=0, has_side_effects=True, vmem_limit_bytes=67043328
+            collective_id=0, has_side_effects=True, vmem_limit_bytes=54848 * 1024
         ),
     )(
         fields.reshape(full), forcing.reshape(full), diffusion, reaction,
-        wrap_factor, mean_diffusion, spectral_shift, high, low, eigen, bands,
+        wrap_factor, mean_diffusion, spectral_shift, tables,
     )
     return result[None, None]
 

time: 63.1 us -> 60.9 us (0.965)
  Pallas kernels: 59.3 us -> 58.1 us
  local copies, waits for them, and re-layouts: 1.67 us -> 0.71 us
    pallas_call x1, Pallas kernels: 59.3 us -> 58.1 us  [on_device(): pl.pallas_call(kernel, out_shape=jax.ShapeDtypeStruct(full, f32), in_spec...]
    unnamed x1, local copies, waits for them, and re-layouts: 1.67 us -> 0.71 us
where the time goes in v4:
time: 60.9 us; the launch traced here: 60.8 us
  Pallas kernels  58.1 us (95%)
  between operations  1.95 us (3%)
  local copies, waits for them, and re-layouts  0.71 us (1%)
    pallas_call x1, Pallas kernels, on_device(): pl.pallas_call(kernel, out_shape=jax.ShapeDtypeStruct(full, f32), in_spec...  58.1 us

profile of v4, /device:TPU:1, one launch (start us, length us, event | category | flops | bytes accessed | tf_op | source)
XLA Modules:
  0.0 60.8 jit_solution(12820651491733913113)
XLA Ops:
  1.9 58.1 %shard_map.82 = f32[256,256]{1,0:T(8,128)S(1)} custom-call(f32[256,256]{1,0:T(8,128)} %bitcast.4, f32[256,256]{1,0:T(8,128)} %bitcast.5, f32[256,256]{1,0:T(8,128)} %diffusion.1, f32[256,256]{1,0:T(8,128)} %reaction.1, f32[1]{0:T(128)S(6)} %copy.10.wrap_in, f32[1]{0:T(128)S(6)} %copy.11.mean_in, f32[1]{0:T(128)S(6)} %copy.12.shift_in, ...), custom_call_target="tpu_custom_call" | custom-call | tf_op jit(solution)/shard_map/pallas_call | solution.py:332
  60.0 0.7 %copy.13 = f32[1,1,256,256]{3,2,1,0:T(8,128)} copy(f32[1,1,256,256]{3,2,1,0:T(8,128)S(1)} %bitcast.3) | data formatting | bytes 524288

commit v5 on v4

--- a/solution.py
+++ b/solution.py
@@ -53,8 +53,8 @@
 
 def kernel(
     fields, forcing, diffusion, reaction, wrap_in, mean_in, shift_in, tables, out, wrap_ref, mean_ref, shift_ref, value, source, diff, react, matrix, high, low, eig, ratio,
-    gain, partner, wrapped, rhs, coef, modes, sibling, part, part_far, joined, arrived, give,
-    carry, in_sems, pair_sems, wrap_sems, part_sems, local_sems, swap_send, swap_recv, out_send,
+    gain, partner, wrapped, rhs, coef, modes, sibling, part, part_far, joined, arrived, give, seed,
+    carry, in_sems, pair_sems, wrap_sems, seed_sems, part_sems, local_sems, swap_send, swap_recv, out_send,
     out_recv, back_send, back_recv, met,
 ):
     group = lax.axis_index("pair")
@@ -82,19 +82,14 @@
     for load in loads:
         load.start()
 
-    is_first = place == (STEPS - 1) * group
     is_last = place == (STEPS - 1) * (1 - group)
-    is_edge = (place == 0) | (place == STEPS - 1)
+    is_beside = (place ^ 1) == (STEPS - 1) * (1 - group)
     barrier = pltpu.get_barrier_semaphore()
 
     def greet(pair, tm):
         pl.semaphore_signal(
             barrier, inc=1, device_id={"pair": pair, "tm": tm}, device_id_type=MESH
         )
-
-    @pl.when(is_edge)
-    def _():
-        greet(group, STEPS - 1 - place)
 
     def chip_at(move_y, move_x, move_z):
         y = (chip // 32 + move_y) % 2
@@ -108,7 +103,7 @@
     greet(1 - group, place)
     for tm in along_z + along_x + along_y + [place ^ 1]:
         greet(group, tm)
-    pl.semaphore_wait(barrier, 10 + is_edge.astype(jnp.int32))
+    pl.semaphore_wait(barrier, 10)
 
     def remote(src, dst, send_sem, recv_sem, pair, tm):
         return pltpu.make_async_remote_copy(
@@ -117,14 +112,7 @@
         )
 
     pair_copy = remote(fields, partner, pair_sems.at[0], pair_sems.at[1], 1 - group, place)
-    wrap_copy = remote(
-        fields, wrapped, wrap_sems.at[0], wrap_sems.at[1], group, STEPS - 1 - place
-    )
     pair_copy.start()
-
-    @pl.when(is_last)
-    def _():
-        wrap_copy.start()
 
     for load in loads:
         load.wait()
@@ -173,7 +161,6 @@
     for _ in range(3):
         full_power = full_power * full_power
     wrap_gain = alpha / (1.0 - alpha * full_power)
-    last = jnp.zeros_like(band_ratio)
     own_rows = pl.ds(pl.multiple_of(core * HALF, HALF), HALF)
 
     other_rows = pl.ds(pl.multiple_of((1 - core) * HALF, HALF), HALF)
@@ -196,17 +183,41 @@
         def _():
             rhs[...] -= 3.0 * cubic * other * other - other
 
+    wrap_copy = remote(
+        wrapped.at[other_rows], wrapped.at[other_rows], wrap_sems.at[0], wrap_sems.at[1], group,
+        place ^ 1,
+    )
+    seed_copies = [
+        remote(
+            wrapped.at[band(chip ^ d, core * HALF)], seed, seed_sems.at[0], seed_sems.at[1],
+            group, place ^ (2 * d),
+        )
+        for d in range(CHIPS - 1, 0, -1)
+    ]
+
+    @pl.when(is_last)
+    def _():
+        wrapped[...] = dot_left(
+            high[...], low[...], dot_right(value[...], high[...], low[...])
+        )
+        wrap_copy.start()
+
+    @pl.when(is_beside)
+    def _():
+        wrap_copy.wait_recv()
+
+    @pl.when(is_last | is_beside)
+    def _():
+        for copy in seed_copies:
+            copy.start()
+        keep = pltpu.make_async_copy(
+            wrapped.at[my_rows, my_lanes], seed, seed_sems.at[2]
+        )
+        keep.start()
+        keep.wait()
+
     pair_copy.wait()
     couple(partner[...])
-
-    @pl.when(is_last)
-    def _():
-        wrap_copy.wait_send()
-
-    @pl.when(is_first)
-    def _():
-        wrap_copy.wait_recv()
-        rhs[...] -= alpha * wrapped[...]
 
     part_copy = remote(part, part_far, part_sems.at[0], part_sems.at[1], 1 - group, place)
 
@@ -250,6 +261,25 @@
         )
         wait.wait_send()
         wait.wait_recv()
+
+        if it == 0:
+
+            @pl.when(is_last)
+            def _():
+                wrap_copy.wait_send()
+
+            @pl.when(is_last | is_beside)
+            def _():
+                remote(
+                    give.at[span], arrived.at[it, span], seed_sems.at[0], seed_sems.at[1], group,
+                    place ^ 1,
+                ).wait_send()
+
+            @pl.when(jnp.logical_not(is_last | is_beside))
+            def _():
+                seed_copies[0].wait_recv()
+
+            last = seed[...]
 
         runs = CHIPS // RUN
         state = [jnp.zeros_like(band_ratio) for _ in range(runs)]
@@ -359,10 +389,12 @@
             pltpu.VMEM(half, f32),
             pltpu.VMEM((ITERS,) + block, f32),
             pltpu.VMEM(block, f32),
+            pltpu.VMEM((SUB, LANES), f32),
             pltpu.VMEM((ITERS, 2) + full, f32),
             pltpu.SemaphoreType.DMA((10,)),
             pltpu.SemaphoreType.DMA((2,)),
             pltpu.SemaphoreType.DMA((2,)),
+            pltpu.SemaphoreType.DMA((3,)),
             pltpu.SemaphoreType.DMA((2,)),
             pltpu.SemaphoreType.DMA((ITERS, 2)),
             pltpu.SemaphoreType.DMA((ITERS, 4)),

time: 60.9 us -> 60.3 us (level)
  no operation moved by 1% of the time
where the time goes in v5:
time: 60.3 us; the launch traced here: 60.2 us
  Pallas kernels  57.6 us (96%)
  between operations  1.95 us (3%)
  local copies, waits for them, and re-layouts  0.71 us (1%)
    pallas_call x1, Pallas kernels, on_device(): pl.pallas_call(kernel, out_shape=jax.ShapeDtypeStruct(full, f32), in_spec...  57.6 us

profile of v5, /device:TPU:1, one launch (start us, length us, event | category | flops | bytes accessed | tf_op | source)
XLA Modules:
  0.0 60.2 jit_solution(164793406708995933)
XLA Ops:
  1.9 57.6 %shard_map.82 = f32[256,256]{1,0:T(8,128)S(1)} custom-call(f32[256,256]{1,0:T(8,128)} %bitcast.4, f32[256,256]{1,0:T(8,128)} %bitcast.5, f32[256,256]{1,0:T(8,128)} %diffusion.1, f32[256,256]{1,0:T(8,128)} %reaction.1, f32[1]{0:T(128)S(6)} %copy.10.wrap_in, f32[1]{0:T(128)S(6)} %copy.11.mean_in, f32[1]{0:T(128)S(6)} %copy.12.shift_in, ...), custom_call_target="tpu_custom_call" | custom-call | tf_op jit(solution)/shard_map/pallas_call | solution.py:362
  59.5 0.7 %copy.13 = f32[1,1,256,256]{3,2,1,0:T(8,128)} copy(f32[1,1,256,256]{3,2,1,0:T(8,128)S(1)} %bitcast.3) | data formatting | bytes 524288

commit v6 on v5

--- a/solution.py
+++ b/solution.py
@@ -18,6 +18,18 @@
 LANES = 128
 RUN = 8
 MESH = pl.DeviceIdType.MESH
+
+
+def ring(move, length):
+    return min(move, length - move)
+
+
+def hops(move):
+    return move[0] + ring(move[1], 4) + ring(move[2], 8)
+
+
+MOVES = [(y, x, z) for y in range(2) for x in range(4) for z in range(8)][1:]
+MOVES.sort(key=lambda move: (-hops(move), -ring(move[2], 8)))
 
 
 def cas_matrix(length):
@@ -91,11 +103,14 @@
             barrier, inc=1, device_id={"pair": pair, "tm": tm}, device_id_type=MESH
         )
 
-    def chip_at(move_y, move_x, move_z):
-        y = (chip // 32 + move_y) % 2
-        x = (chip // 8 + move_x) % 4
-        z = (chip + move_z) % 8
-        return 2 * (32 * y + 8 * x + z) + core
+    def peer_at(move):
+        y = (chip // 32 + move[0]) % 2
+        x = (chip // 8 + move[1]) % 4
+        z = (chip + move[2]) % 8
+        return 32 * y + 8 * x + z
+
+    def chip_at(*move):
+        return 2 * peer_at(move) + core
 
     along_z = [chip_at(0, 0, move) for move in (1, 7, 2, 6)]
     along_x = [chip_at(0, move, 0) for move in (1, 2, 3)]
@@ -189,10 +204,10 @@
     )
     seed_copies = [
         remote(
-            wrapped.at[band(chip ^ d, core * HALF)], seed, seed_sems.at[0], seed_sems.at[1],
-            group, place ^ (2 * d),
-        )
-        for d in range(CHIPS - 1, 0, -1)
+            wrapped.at[band(peer_at(move), core * HALF)], seed, seed_sems.at[0],
+            seed_sems.at[1], group, chip_at(*move),
+        )
+        for move in MOVES
     ]
 
     @pl.when(is_last)
@@ -238,12 +253,12 @@
         near, beside = modes[it, own_rows], sibling[it, own_rows]
         q = ratio[own_rows]
         joined[...] = q * jnp.where(own_first, q * near + beside, q * beside + near)
-        for d in range(CHIPS - 1, 0, -1):
-            peer = chip ^ d
+        for move in MOVES:
+            peer = peer_at(move)
             rows, lanes = band(peer, 0)
             remote(
                 joined.at[rows, lanes], arrived.at[it, chip], out_send.at[it], out_recv.at[it],
-                group, place ^ (2 * d),
+                group, 2 * peer + core,
             ).start()
         rows, lanes = band(chip, 0)
         keep = pltpu.make_async_copy(
@@ -303,17 +318,17 @@
                 give[n] += enters[b]
                 enters[b] = pair_ratio * enters[b]
 
-        for d in range(CHIPS - 1, -1, -1):
-            peer = chip ^ d
+        for move in MOVES + [(0, 0, 0)]:
+            peer = peer_at(move)
             if not final:
                 remote(
                     give.at[peer], carry.at[it, 1, my_rows, my_lanes], back_send.at[it, 1],
-                    back_recv.at[it, 1], 1 - group, place ^ (2 * d),
+                    back_recv.at[it, 1], 1 - group, 2 * peer + core,
                 ).start()
-            if d:
+            if any(move):
                 remote(
                     give.at[peer], carry.at[it, 0, my_rows, my_lanes], back_send.at[it, 0],
-                    back_recv.at[it, 0], group, place ^ (2 * d),
+                    back_recv.at[it, 0], group, 2 * peer + core,
                 ).start()
         keep = pltpu.make_async_copy(
             give.at[chip], carry.at[it, 0, my_rows, my_lanes], local_sems.at[it, 1]

time: 60.3 us -> 58.7 us (0.973)
  Pallas kernels: 57.6 us -> 55.9 us
    pallas_call x1, Pallas kernels: 57.6 us -> 55.9 us  [on_device(): pl.pallas_call(kernel, out_shape=jax.ShapeDtypeStruct(full, f32), in_spec...]
where the time goes in v6:
time: 58.7 us; the launch traced here: 58.6 us
  Pallas kernels  55.9 us (95%)
  between operations  1.95 us (3%)
  local copies, waits for them, and re-layouts  0.71 us (1%)
    pallas_call x1, Pallas kernels, on_device(): pl.pallas_call(kernel, out_shape=jax.ShapeDtypeStruct(full, f32), in_spec...  55.9 us

profile of v6, /device:TPU:1, one launch (start us, length us, event | category | flops | bytes accessed | tf_op | source)
XLA Modules:
  0.0 58.6 jit_solution(4101452253438809511)
XLA Ops:
  1.9 55.9 %shard_map.82 = f32[256,256]{1,0:T(8,128)S(1)} custom-call(f32[256,256]{1,0:T(8,128)} %bitcast.4, f32[256,256]{1,0:T(8,128)} %bitcast.5, f32[256,256]{1,0:T(8,128)} %diffusion.1, f32[256,256]{1,0:T(8,128)} %reaction.1, f32[1]{0:T(128)S(6)} %copy.10.wrap_in, f32[1]{0:T(128)S(6)} %copy.11.mean_in, f32[1]{0:T(128)S(6)} %copy.12.shift_in, ...), custom_call_target="tpu_custom_call" | custom-call | tf_op jit(solution)/shard_map/pallas_call | solution.py:377
  57.9 0.7 %copy.13 = f32[1,1,256,256]{3,2,1,0:T(8,128)} copy(f32[1,1,256,256]{3,2,1,0:T(8,128)S(1)} %bitcast.3) | data formatting | bytes 524288

commit v7 on v6

--- a/solution.py
+++ b/solution.py
@@ -268,6 +268,8 @@
         swaps[1].wait()
         near = modes[it]
         part[...] = ratio[...] * jnp.where(own_first, near, near + ratio[...] * sibling[it])
+        if not final:
+            part_copy.start()
         keep.wait()
         span = pl.ds(0, CHIPS - 1)
         wait = remote(
@@ -335,8 +337,6 @@
         )
         keep.start()
         keep.wait()
-        if not final:
-            part_copy.start()
         kinds = 1 if final else 2
         swaps = []
         for kind in range(kinds):

time: 58.7 us -> 57.9 us (0.986)
  Pallas kernels: 55.9 us -> 55.1 us
    pallas_call x1, Pallas kernels: 55.9 us -> 55.1 us  [on_device(): pl.pallas_call(kernel, out_shape=jax.ShapeDtypeStruct(full, f32), in_spec...]
where the time goes in v7:
time: 57.9 us; the launch traced here: 57.8 us
  Pallas kernels  55.1 us (95%)
  between operations  1.95 us (3%)
  local copies, waits for them, and re-layouts  0.71 us (1%)
    pallas_call x1, Pallas kernels, on_device(): pl.pallas_call(kernel, out_shape=jax.ShapeDtypeStruct(full, f32), in_spec...  55.1 us

profile of v7, /device:TPU:1, one launch (start us, length us, event | category | flops | bytes accessed | tf_op | source)
XLA Modules:
  0.0 57.8 jit_solution(2139889203776144383)
XLA Ops:
  1.9 55.1 %shard_map.82 = f32[256,256]{1,0:T(8,128)S(1)} custom-call(f32[256,256]{1,0:T(8,128)} %bitcast.4, f32[256,256]{1,0:T(8,128)} %bitcast.5, f32[256,256]{1,0:T(8,128)} %diffusion.1, f32[256,256]{1,0:T(8,128)} %reaction.1, f32[1]{0:T(128)S(6)} %copy.10.wrap_in, f32[1]{0:T(128)S(6)} %copy.11.mean_in, f32[1]{0:T(128)S(6)} %copy.12.shift_in, ...), custom_call_target="tpu_custom_call" | custom-call | tf_op jit(solution)/shard_map/pallas_call | solution.py:377
  57.1 0.7 %copy.13 = f32[1,1,256,256]{3,2,1,0:T(8,128)} copy(f32[1,1,256,256]{3,2,1,0:T(8,128)S(1)} %bitcast.3) | data formatting | bytes 524288
